TPU v7x, 256 devices: a whole 4x4x8 slice. The times are simulated.
256 devices in a mesh: rows: 32 (over x, z), vecs: 8 (over y, core).
Axes of the slice: x: 4, y: 4, z: 8, core: 2. Of those that a mesh axis runs over, the one named last changes fastest.
Arguments:
- coords: float32 [3, 8192], P(None, ('rows', 'vecs')), may hold values from 0 to 1
- old_vectors: bfloat16 [8192, 16384], P('rows', 'vecs'), may hold values from -0.078125 to 0.078125
- pivots: int32 [2, 128], replicated, may hold values from 0 to 8191, as said below
- slots: int32 [8192], replicated, may hold values from 0 to 8191, each once
Outputs:
- new_vectors: float32 [8192, 256], P(('rows', 'vecs'))
Inputs may be any that keep to these rules, and one draw needn't show every extreme that they name: `pivots`: all 256 pivot numbers are distinct. `slots`: each window row belongs to exactly one point.
All inputs are finite; a program needn't handle non-finite values.
Results may differ from a plain program's by a relative error of at most 0.0003.
Values may be sent and summed in bfloat16 or wider, within the bound.
A program may use at most 64 MiB of HBM per device.

v0:
```python
import jax
import jax.numpy as jnp
from jax import lax
from jax.sharding import PartitionSpec as P

length_scale = 0.5
noise_shift = 12.0


def matern(points, centers):
    dist_sq = jnp.zeros((points.shape[1], centers.shape[1]), jnp.float32)
    for component in range(3):
        differ = points[component][:, None] - centers[component][None, :]
        dist_sq = dist_sq + differ * differ
    scaled = jnp.sqrt(5.0 * dist_sq) / length_scale
    return (1.0 + scaled + scaled * scaled / 3.0) * jnp.exp(-scaled)


def pick_rows(block_data, wanted, first_row):
    length = block_data.shape[0]
    offset = wanted - first_row
    inside = (offset >= 0) & (offset < length)
    bounded = jnp.clip(offset, 0, length - 1)
    fetched = jnp.take(block_data, bounded, axis=0)
    return jnp.where(inside[:, None], fetched, jnp.zeros((), block_data.dtype))


def shards(coords, old_vectors, pivots, slots):
    row_block = old_vectors.shape[0]
    share = coords.shape[1]
    panels = pivots.shape[0]
    width = pivots.shape[1]
    block_first = lax.axis_index("rows") * row_block
    share_first = block_first + lax.axis_index("vecs") * share
    wanted = jnp.take(slots, pivots.reshape(-1), axis=0)
    my_rows = share_first + jnp.arange(share, dtype=jnp.int32)
    every_point = lax.all_gather(coords, ("rows", "vecs"), axis=1, tiled=True)
    centers = jnp.take(every_point, wanted, axis=1)
    new_panels = []
    for panel in range(panels):
        chosen = wanted[panel * width : (panel + 1) * width]
        old_pivot = (
            lax.psum(pick_rows(old_vectors, chosen, block_first), "rows")
            .astype(jnp.float32)
            .astype(jnp.bfloat16)
        )

        def residual_term(first_row, length, old_pivot=old_pivot):
            return jnp.dot(old_vectors, old_pivot.T, preferred_element_type=jnp.float32)

        summed = lax.psum_scatter(
            residual_term(jnp.int32(0), share * lax.axis_size("vecs")),
            "vecs",
            scatter_dimension=0,
            tiled=True,
        )
        kernel = matern(coords, centers[:, panel * width : (panel + 1) * width])
        kernel = kernel + noise_shift * (my_rows[:, None] == chosen[None, :]).astype(jnp.float32)
        current = kernel - summed
        if panel > 0:
            stacked = new_panels[0]
            earlier = lax.psum(pick_rows(stacked, chosen, share_first), ("rows", "vecs"))
            current = current - jnp.dot(
                stacked,
                earlier.T,
                precision=lax.Precision.HIGHEST,
                preferred_element_type=jnp.float32,
            )
        block = lax.psum(pick_rows(current, chosen, share_first), ("rows", "vecs"))
        factor = jnp.linalg.cholesky(block)
        fresh = jax.scipy.linalg.solve_triangular(factor, current.T, lower=True).T
        new_panels.append(fresh)
    return jnp.concatenate(new_panels, axis=1)


def solution(mesh):
    in_specs = (P(None, ("rows", "vecs")), P("rows", "vecs"), P(), P())
    out_specs = P(("rows", "vecs"), None)
    return jax.shard_map(shards, mesh=mesh, in_specs=in_specs, out_specs=out_specs, check_vma=False)
```

profile of v0, /device:TPU:1, one launch (start us, length us, event | category | flops | bytes accessed | tf_op | source)
XLA Modules:
  0.0 1000.4 jit_solution(14306244718149790146)
XLA Ops:
  6.5 0.8 compare_select_fusion.1
  7.3 2.0 gather_fusion
  9.3 0.7 compare_and_fusion.7
  10.1 0.9 gather_fusion.4
  11.0 0.9 gather_fusion.2
  12.0 1.2 select_select_fusion
  13.2 73.2 %all-gather = f32[256,32,3]{1,2,0:T(4,128)S(1)} all-gather(f32[1,32,3]{1,2,0:T(4,128)S(1)} %bitcast.66), channel_id=1, replica_groups=mesh['rows'=32,'vecs'=8] {'rows','vecs'}, dimensions={0}, use_global_device_ids=true | all-gather | bytes 98688 | tf_op jit(solution)/shard_map/all_gather | solution.py:37
  86.5 3.0 copy.23
  89.5 2.9 gather_fusion.1
  92.8 70.1 %all-reduce.12.cloned.1.call-done = (bf16[128,2048]{1,0:T(8,128)(2,1)}, bf16[128,2048]{1,0:T(8,128)(2,1)}) async-done(((bf16[128,2048]{1,0:T(8,128)(2,1)}, bf16[128,2048]{1,0:T(8,128)(2,1)}), (bf16[128,2048]{1,0:T(8,128)(2,1)}, bf16[128,2048]{1,0:T(8,128)(2,1)})) %all-reduce.12.cloned.1.call-update) | async-done | bytes 1048592 | tf_op jit(solution)/shard_map/psum | solution.py:43
  162.9 1.5 convolution_bitcast_fusion.1
  164.4 0.7 copy.31
  165.3 33.3 %reduce-scatter.7.cloned.1.call-done = f32[32,128]{1,0:T(8,128)} async-done(((f32[256,128]{1,0:T(8,128)}), f32[32,128]{1,0:T(8,128)}) %reduce-scatter.7.cloned.1.call-update) | async-done | bytes 16400 | tf_op jit(solution)/shard_map/reduce_scatter | solution.py:51
  198.5 0.8 add_subtract_fusion
  200.8 1.5 convolution_bitcast_fusion
  202.3 0.7 copy.33
  203.1 243.7 %all-reduce.6.cloned.1.call-done = f32[128,128]{0,1:T(8,128)} async-done(((f32[128,128]{0,1:T(8,128)}), f32[128,128]{0,1:T(8,128)}) %all-reduce.6.cloned.1.call-update) | async-done | bytes 65552 | tf_op jit(solution)/shard_map/psum | solution.py:69
  446.9 0.9 copy.26
  447.8 0.9 fusion.6
  448.6 11.7 %cholesky.44 = f32[128,128]{1,0:T(8,128)S(1)} custom-call(f32[128,128]{1,0:T(8,128)S(1)} %fusion.6), custom_call_target="Cholesky" | custom-call | tf_op jit(solution)/shard_map/jit(cholesky)/cholesky | solution.py:70
  461.0 0.7 fusion
  461.7 9.8 custom-call.6
  471.7 0.7 gather_fusion.5
  473.3 3.4 reduce-scatter.9.cloned.1.call-done
  476.7 248.0 %all-reduce.8.cloned.1.call-done = f32[128,128]{0,1:T(8,128)} async-done(((f32[128,128]{0,1:T(8,128)}), f32[128,128]{0,1:T(8,128)}) %all-reduce.8.cloned.1.call-update) | async-done | bytes 65552 | tf_op jit(solution)/shard_map/psum | solution.py:62
  724.8 1.0 convolution_subtract_fusion
  727.2 240.9 %all-reduce.10.cloned.1.call-done = f32[128,128]{0,1:T(8,128)} async-done(((f32[128,128]{0,1:T(8,128)}), f32[128,128]{0,1:T(8,128)}) %all-reduce.10.cloned.1.call-update) | async-done | bytes 65552 | tf_op jit(solution)/shard_map/psum | solution.py:69
  968.1 0.9 copy.30
  969.0 0.9 fusion.3
  969.9 11.7 %cholesky.55 = f32[128,128]{1,0:T(8,128)S(1)} custom-call(f32[128,128]{1,0:T(8,128)S(1)} %fusion.3), custom_call_target="Cholesky" | custom-call | tf_op jit(solution)/shard_map/jit(cholesky)/cholesky | solution.py:70
  982.3 0.7 fusion.1
  983.0 9.8 custom-call.7
  (46 shorter events, 6.7 us)
Async XLA Ops:
  6.5 3.5 copy-start
  6.5 156.3 %all-reduce.12.cloned.1.call-start = ((), (), s32[]{:S(2)}) async-start(), calls=%async_computation.7 | async-start | bytes 2097152 | tf_op jit(solution)/shard_map/psum | solution.py:43
  11.0 2.2 copy-start.2
  12.0 77.5 %copy-start.1 = (s32[2,128]{1,0:T(2,128)S(1)}, s32[2,128]{1,0:T(2,128)}, u32[]{:S(2)}) copy-start(s32[2,128]{1,0:T(2,128)} %param.13) | copy-start | bytes 3076
  13.2 185.3 %reduce-scatter.7.cloned.1.call-start = ((), (), s32[]{:S(2)}) async-start(), calls=%async_computation.5 | async-start | bytes 147456 | tf_op jit(solution)/shard_map/reduce_scatter | solution.py:51
  165.2 281.7 %all-reduce.6.cloned.1.call-start = ((), (), s32[]{:S(2)}) async-start(), calls=%async_computation.2 | async-start | bytes 131072 | tf_op jit(solution)/shard_map/psum | solution.py:69
  200.7 276.0 %reduce-scatter.9.cloned.1.call-start = ((), (), s32[]{:S(2)}) async-start(), calls=%async_computation.6 | async-start | bytes 147456 | tf_op jit(solution)/shard_map/reduce_scatter | solution.py:51
  203.1 521.7 %all-reduce.8.cloned.1.call-start = ((), (), s32[]{:S(2)}) async-start(), calls=%async_computation.3 | async-start | bytes 131072 | tf_op jit(solution)/shard_map/psum | solution.py:62
  473.1 495.0 %all-reduce.10.cloned.1.call-start = ((), (), s32[]{:S(2)}) async-start(), calls=%async_computation.4 | async-start | bytes 131072 | tf_op jit(solution)/shard_map/psum | solution.py:69
Sparse Core Ops, SparseCore 0:
  13.3 149.5 all-reduce.11
  165.4 33.0 reduce-scatter.6
  204.0 242.7 all-reduce.5
  449.2 27.4 reduce-scatter.8
  482.1 242.6 all-reduce.7
  730.2 237.9 all-reduce.9
where the time goes:
time: 1000 us
  waiting for transfers between devices  840 us (84%)
  blocking collectives  73.2 us (7%)
  other arithmetic  53.6 us (5%)
  local copies, waits for them, and re-layouts  15.6 us (2%)
  between operations  13.7 us (1%)
    psum x2, waiting for transfers between devices, shards(): block = lax.psum(pick_rows(current, chosen, share_first), ('rows', 'vecs'))  485 us
    psum x1, waiting for transfers between devices, shards(): lax.psum(pick_rows(stacked, chosen, share_first), ('rows', 'vecs'))  248 us
    all_gather x1, blocking collectives, shards(): every_point = lax.all_gather(coords, ('rows', 'vecs'), axis=1, tiled=True)  73.2 us
    psum x1, waiting for transfers between devices, shards(): lax.psum(pick_rows(old_vectors, chosen, block_first), 'rows')  70.1 us
    reduce_scatter x2, waiting for transfers between devices, shards(): lax.psum_scatter(residual_term(jnp.int32(0), share * lax.axis_size('vecs'...  36.7 us
    another operation x6, other arithmetic, shards(): factor = jnp.linalg.cholesky(block)  24.8 us
    another operation x4, other arithmetic, shards(): fresh = jax.scipy.linalg.solve_triangular(factor, current.T, lower=True).T  20.9 us
  transfers between devices with their start and end apart: 6, of which 6 were waited for; matrix products, arithmetic and copies ran while one was open for 3% of the time, Pallas kernels for 0%

commit v1 on v0

--- a/solution.py
+++ b/solution.py
@@ -66,7 +66,7 @@
                 precision=lax.Precision.HIGHEST,
                 preferred_element_type=jnp.float32,
             )
-        block = lax.psum(pick_rows(current, chosen, share_first), ("rows", "vecs"))
+        block = lax.psum(lax.psum(pick_rows(current, chosen, share_first), "rows"), "vecs")
         factor = jnp.linalg.cholesky(block)
         fresh = jax.scipy.linalg.solve_triangular(factor, current.T, lower=True).T
         new_panels.append(fresh)

time: 1000 us -> 929 us (0.929)
  waiting for transfers between devices: 840 us -> 766 us
    psum x2 -> x4, waiting for transfers between devices: 485 us -> 406 us  [the longest x2 273 us: shards(): lax.psum(pick_rows(current, chosen, share_first), 'rows')]
  transfers between devices with their start and end apart: 6 -> 8, of which waited for: 6 -> 8; matrix products, arithmetic and copies ran while one was open for 3% -> 4% of each run, Pallas kernels for 0% -> 0%
where the time goes in v1:
time: 929 us; the launch traced here: 927 us
  waiting for transfers between devices  766 us (82%)
  blocking collectives  73.2 us (8%)
  other arithmetic  53.6 us (6%)
  local copies, waits for them, and re-layouts  15.6 us (2%)
  between operations  13.7 us (1%)
    psum x2, waiting for transfers between devices, shards(): lax.psum(pick_rows(current, chosen, share_first), 'rows')  273 us
    psum x1, waiting for transfers between devices, shards(): lax.psum(pick_rows(stacked, chosen, share_first), ('rows', 'vecs'))  248 us
    psum x2, waiting for transfers between devices, shards(): lax.psum(lax.psum(pick_rows(current, chosen, share_first), 'rows'), 'vecs')  133 us
    all_gather x1, blocking collectives, shards(): every_point = lax.all_gather(coords, ('rows', 'vecs'), axis=1, tiled=True)  73.2 us
    psum x1, waiting for transfers between devices, shards(): lax.psum(pick_rows(old_vectors, chosen, block_first), 'rows')  70.1 us
    reduce_scatter x2, waiting for transfers between devices, shards(): lax.psum_scatter(residual_term(jnp.int32(0), share * lax.axis_size('vecs'...  41.7 us
    another operation x6, other arithmetic, shards(): factor = jnp.linalg.cholesky(block)  24.8 us
    another operation x4, other arithmetic, shards(): fresh = jax.scipy.linalg.solve_triangular(factor, current.T, lower=True).T  20.9 us
  transfers between devices with their start and end apart: 8, of which 8 were waited for; matrix products, arithmetic and copies ran while one was open for 4% of the time, Pallas kernels for 0%

profile of v1, /device:TPU:1, one launch (start us, length us, event | category | flops | bytes accessed | tf_op | source)
XLA Modules:
  0.0 927.4 jit_solution(8206328812932801323)
XLA Ops:
  6.5 0.8 compare_select_fusion.1
  7.3 2.0 gather_fusion
  9.3 0.7 compare_and_fusion.7
  10.1 0.9 gather_fusion.4
  11.0 0.9 gather_fusion.2
  12.0 1.2 select_select_fusion
  13.2 73.2 %all-gather = f32[256,32,3]{1,2,0:T(4,128)S(1)} all-gather(f32[1,32,3]{1,2,0:T(4,128)S(1)} %bitcast.66), channel_id=1, replica_groups=mesh['rows'=32,'vecs'=8] {'rows','vecs'}, dimensions={0}, use_global_device_ids=true | all-gather | bytes 98688 | tf_op jit(solution)/shard_map/all_gather | solution.py:37
  86.5 3.0 copy.23
  89.5 2.9 gather_fusion.1
  92.8 70.1 %all-reduce.18.cloned.1.call-done = (bf16[128,2048]{1,0:T(8,128)(2,1)}, bf16[128,2048]{1,0:T(8,128)(2,1)}) async-done(((bf16[128,2048]{1,0:T(8,128)(2,1)}, bf16[128,2048]{1,0:T(8,128)(2,1)}), (bf16[128,2048]{1,0:T(8,128)(2,1)}, bf16[128,2048]{1,0:T(8,128)(2,1)})) %all-reduce.18.cloned.1.call-update) | async-done | bytes 1048592 | tf_op jit(solution)/shard_map/psum | solution.py:43
  162.9 1.5 convolution_bitcast_fusion.1
  164.4 0.7 copy.31
  165.3 33.3 %reduce-scatter.7.cloned.1.call-done = f32[32,128]{1,0:T(8,128)} async-done(((f32[256,128]{1,0:T(8,128)}), f32[32,128]{1,0:T(8,128)}) %reduce-scatter.7.cloned.1.call-update) | async-done | bytes 16400 | tf_op jit(solution)/shard_map/reduce_scatter | solution.py:51
  198.5 0.8 add_subtract_fusion
  200.8 139.3 %all-reduce.8.cloned.1.call-done = f32[128,128]{0,1:T(8,128)} async-done(((f32[128,128]{0,1:T(8,128)}), f32[128,128]{0,1:T(8,128)}) %all-reduce.8.cloned.1.call-update) | async-done | bytes 65552 | tf_op jit(solution)/shard_map/psum | solution.py:69
  340.2 1.5 convolution_bitcast_fusion
  341.7 0.7 copy.33
  342.5 65.2 %all-reduce.10.cloned.1.call-done = f32[128,128]{0,1:T(8,128)} async-done(((f32[128,128]{0,1:T(8,128)}), f32[128,128]{0,1:T(8,128)}) %all-reduce.10.cloned.1.call-update) | async-done | bytes 65552 | tf_op jit(solution)/shard_map/psum | solution.py:69
  407.7 0.9 copy.26
  408.7 0.9 fusion.6
  409.5 11.7 %cholesky.44 = f32[128,128]{1,0:T(8,128)S(1)} custom-call(f32[128,128]{1,0:T(8,128)S(1)} %fusion.6), custom_call_target="Cholesky" | custom-call | tf_op jit(solution)/shard_map/jit(cholesky)/cholesky | solution.py:70
  421.9 0.7 fusion
  422.6 9.8 %custom-call.6 = f32[1,128,128]{1,2,0:T(8,128)S(1)} custom-call(f32[1,128,128]{2,1,0:T(8,128)S(1)} %fusion), custom_call_target="InvertDiagBlocksLowerTriangular" | custom-call | tf_op jit(solution)/shard_map/jit(_solve_triangular)/triangular_solve | solution.py:71
  434.0 8.4 reduce-scatter.9.cloned.1.call-done
  442.4 248.2 %all-reduce.12.cloned.1.call-done = f32[128,128]{0,1:T(8,128)} async-done(((f32[128,128]{0,1:T(8,128)}), f32[128,128]{0,1:T(8,128)}) %all-reduce.12.cloned.1.call-update) | async-done | bytes 65552 | tf_op jit(solution)/shard_map/psum | solution.py:62
  690.7 1.0 convolution_subtract_fusion
  693.3 134.0 %all-reduce.14.cloned.1.call-done = f32[128,128]{0,1:T(8,128)} async-done(((f32[128,128]{0,1:T(8,128)}), f32[128,128]{0,1:T(8,128)}) %all-reduce.14.cloned.1.call-update) | async-done | bytes 65552 | tf_op jit(solution)/shard_map/psum | solution.py:69
  827.4 67.7 %all-reduce.16.cloned.1.call-done = f32[128,128]{0,1:T(8,128)} async-done(((f32[128,128]{0,1:T(8,128)}), f32[128,128]{0,1:T(8,128)}) %all-reduce.16.cloned.1.call-update) | async-done | bytes 65552 | tf_op jit(solution)/shard_map/psum | solution.py:69
  895.1 0.9 copy.30
  896.0 0.9 fusion.3
  896.9 11.7 %cholesky.55 = f32[128,128]{1,0:T(8,128)S(1)} custom-call(f32[128,128]{1,0:T(8,128)S(1)} %fusion.3), custom_call_target="Cholesky" | custom-call | tf_op jit(solution)/shard_map/jit(cholesky)/cholesky | solution.py:70
  909.9 9.8 %custom-call.7 = f32[1,128,128]{1,2,0:T(8,128)S(1)} custom-call(f32[1,128,128]{2,1,0:T(8,128)S(1)} %fusion.1), custom_call_target="InvertDiagBlocksLowerTriangular" | custom-call | tf_op jit(solution)/shard_map/jit(_solve_triangular)/triangular_solve | solution.py:71
  (52 shorter events, 8.2 us)
Async XLA Ops:
  6.5 3.5 copy-start
  6.5 156.3 %all-reduce.18.cloned.1.call-start = ((), (), s32[]{:S(2)}) async-start(), calls=%async_computation.9 | async-start | bytes 2097152 | tf_op jit(solution)/shard_map/psum | solution.py:43
  11.0 2.2 copy-start.2
  12.0 77.5 %copy-start.1 = (s32[2,128]{1,0:T(2,128)S(1)}, s32[2,128]{1,0:T(2,128)}, u32[]{:S(2)}) copy-start(s32[2,128]{1,0:T(2,128)} %param.13) | copy-start | bytes 3076
  13.2 185.3 %reduce-scatter.7.cloned.1.call-start = ((), (), s32[]{:S(2)}) async-start(), calls=%async_computation.7 | async-start | bytes 147456 | tf_op jit(solution)/shard_map/reduce_scatter | solution.py:51
  165.2 174.9 %all-reduce.8.cloned.1.call-start = ((), (), s32[]{:S(2)}) async-start(), calls=%async_computation.2 | async-start | bytes 131072 | tf_op jit(solution)/shard_map/psum | solution.py:69
  200.7 207.0 %all-reduce.10.cloned.1.call-start = ((), (), s32[]{:S(2)}) async-start(), calls=%async_computation.3 | async-start | bytes 131072 | tf_op jit(solution)/shard_map/psum | solution.py:69
  340.1 102.3 %reduce-scatter.9.cloned.1.call-start = ((), (), s32[]{:S(2)}) async-start(), calls=%async_computation.8 | async-start | bytes 147456 | tf_op jit(solution)/shard_map/reduce_scatter | solution.py:51
  342.5 348.2 %all-reduce.12.cloned.1.call-start = ((), (), s32[]{:S(2)}) async-start(), calls=%async_computation.4 | async-start | bytes 131072 | tf_op jit(solution)/shard_map/psum | solution.py:62
  434.0 393.4 %all-reduce.14.cloned.1.call-start = ((), (), s32[]{:S(2)}) async-start(), calls=%async_computation.5 | async-start | bytes 131072 | tf_op jit(solution)/shard_map/psum | solution.py:69
  693.1 202.0 %all-reduce.16.cloned.1.call-start = ((), (), s32[]{:S(2)}) async-start(), calls=%async_computation.6 | async-start | bytes 131072 | tf_op jit(solution)/shard_map/psum | solution.py:69
Sparse Core Ops, SparseCore 0:
  13.3 149.5 all-reduce.17
  165.4 33.0 reduce-scatter.6
  202.0 138.1 all-reduce.7
  342.3 65.3 all-reduce.9
  410.1 32.3 reduce-scatter.8
  447.8 242.8 all-reduce.11
  694.1 133.1 all-reduce.13
  829.7 65.3 all-reduce.15

commit v2 on v0

--- a/solution.py
+++ b/solution.py
@@ -59,7 +59,7 @@
         current = kernel - summed
         if panel > 0:
             stacked = new_panels[0]
-            earlier = lax.psum(pick_rows(stacked, chosen, share_first), ("rows", "vecs"))
+            earlier = lax.psum(lax.psum(pick_rows(stacked, chosen, share_first), "rows"), "vecs")
             current = current - jnp.dot(
                 stacked,
                 earlier.T,

time: 1000 us -> 990 us (0.990)
  waiting for transfers between devices: 840 us -> 829 us
    psum x1 -> x2, waiting for transfers between devices: 248 us -> 198 us  [the longest x1 132 us: shards(): lax.psum(pick_rows(stacked, chosen, share_first), 'rows')]
    reduce_scatter x2, waiting for transfers between devices: 36.7 us -> 68.9 us  [shards(): lax.psum_scatter(residual_term(jnp.int32(0), share * lax.axis_size('vecs'...]
  transfers between devices with their start and end apart: 6 -> 7, of which waited for: 6 -> 7; matrix products, arithmetic and copies ran while one was open for 3% -> 1% of each run, Pallas kernels for 0% -> 0%
where the time goes in v2:
time: 990 us; the launch traced here: 989 us
  waiting for transfers between devices  829 us (84%)
  blocking collectives  73.2 us (7%)
  other arithmetic  53.6 us (5%)
  local copies, waits for them, and re-layouts  15.6 us (2%)
  between operations  13.7 us (1%)
    psum x2, waiting for transfers between devices, shards(): block = lax.psum(pick_rows(current, chosen, share_first), ('rows', 'vecs'))  492 us
    psum x1, waiting for transfers between devices, shards(): lax.psum(pick_rows(stacked, chosen, share_first), 'rows')  132 us
    all_gather x1, blocking collectives, shards(): every_point = lax.all_gather(coords, ('rows', 'vecs'), axis=1, tiled=True)  73.2 us
    psum x1, waiting for transfers between devices, shards(): lax.psum(pick_rows(old_vectors, chosen, block_first), 'rows')  70.1 us
    reduce_scatter x2, waiting for transfers between devices, shards(): lax.psum_scatter(residual_term(jnp.int32(0), share * lax.axis_size('vecs'...  68.9 us
    psum x1, waiting for transfers between devices, shards(): lax.psum(lax.psum(pick_rows(stacked, chosen, share_first), 'rows'), 'vecs')  66.1 us
    another operation x6, other arithmetic, shards(): factor = jnp.linalg.cholesky(block)  24.8 us
    another operation x4, other arithmetic, shards(): fresh = jax.scipy.linalg.solve_triangular(factor, current.T, lower=True).T  20.9 us
  transfers between devices with their start and end apart: 7, of which 7 were waited for; matrix products, arithmetic and copies ran while one was open for 1% of the time, Pallas kernels for 0%

profile of v2, /device:TPU:1, one launch (start us, length us, event | category | flops | bytes accessed | tf_op | source)
XLA Modules:
  0.0 989.3 jit_solution(2948837148954142427)
XLA Ops:
  6.5 0.8 compare_select_fusion.1
  7.3 2.0 gather_fusion
  9.3 0.7 compare_and_fusion.7
  10.1 0.9 gather_fusion.4
  11.0 0.9 gather_fusion.2
  12.0 1.2 select_select_fusion
  13.2 73.2 %all-gather = f32[256,32,3]{1,2,0:T(4,128)S(1)} all-gather(f32[1,32,3]{1,2,0:T(4,128)S(1)} %bitcast.66), channel_id=1, replica_groups=mesh['rows'=32,'vecs'=8] {'rows','vecs'}, dimensions={0}, use_global_device_ids=true | all-gather | bytes 98688 | tf_op jit(solution)/shard_map/all_gather | solution.py:37
  86.5 3.0 copy.23
  89.5 2.9 gather_fusion.1
  92.8 70.1 %all-reduce.15.cloned.1.call-done = (bf16[128,2048]{1,0:T(8,128)(2,1)}, bf16[128,2048]{1,0:T(8,128)(2,1)}) async-done(((bf16[128,2048]{1,0:T(8,128)(2,1)}, bf16[128,2048]{1,0:T(8,128)(2,1)}), (bf16[128,2048]{1,0:T(8,128)(2,1)}, bf16[128,2048]{1,0:T(8,128)(2,1)})) %all-reduce.15.cloned.1.call-update) | async-done | bytes 1048592 | tf_op jit(solution)/shard_map/psum | solution.py:43
  162.9 1.6 convolution_bitcast_fusion.1
  164.5 0.7 copy.31
  165.3 33.2 %reduce-scatter.7.cloned.1.call-done = f32[32,128]{1,0:T(8,128)} async-done(((f32[256,128]{1,0:T(8,128)}), f32[32,128]{1,0:T(8,128)}) %reduce-scatter.7.cloned.1.call-update) | async-done | bytes 16400 | tf_op jit(solution)/shard_map/reduce_scatter | solution.py:51
  198.5 0.8 add_subtract_fusion
  200.8 246.1 %all-reduce.7.cloned.1.call-done = f32[128,128]{0,1:T(8,128)} async-done(((f32[128,128]{0,1:T(8,128)}), f32[128,128]{0,1:T(8,128)}) %all-reduce.7.cloned.1.call-update) | async-done | bytes 65552 | tf_op jit(solution)/shard_map/psum | solution.py:69
  446.9 0.9 copy.26
  447.8 0.9 fusion.6
  448.7 11.7 %cholesky.44 = f32[128,128]{1,0:T(8,128)S(1)} custom-call(f32[128,128]{1,0:T(8,128)S(1)} %fusion.6), custom_call_target="Cholesky" | custom-call | tf_op jit(solution)/shard_map/jit(cholesky)/cholesky | solution.py:70
  461.1 0.7 fusion
  461.7 9.8 custom-call.6
  471.7 0.7 gather_fusion.5
  473.7 0.7 copy.33
  474.5 132.0 %all-reduce.9.cloned.1.call-done = f32[128,128]{0,1:T(8,128)} async-done(((f32[128,128]{0,1:T(8,128)}), f32[128,128]{0,1:T(8,128)}) %all-reduce.9.cloned.1.call-update) | async-done | bytes 65552 | tf_op jit(solution)/shard_map/psum | solution.py:62
  606.7 35.7 %reduce-scatter.9.cloned.1.call-done = f32[32,128]{1,0:T(8,128)} async-done(((f32[256,128]{1,0:T(8,128)}), f32[32,128]{1,0:T(8,128)}) %reduce-scatter.9.cloned.1.call-update) | async-done | bytes 16400 | tf_op jit(solution)/shard_map/reduce_scatter | solution.py:51
  642.5 66.1 %all-reduce.11.cloned.1.call-done = f32[128,128]{0,1:T(8,128)} async-done(((f32[128,128]{0,1:T(8,128)}), f32[128,128]{0,1:T(8,128)}) %all-reduce.11.cloned.1.call-update) | async-done | bytes 65552 | tf_op jit(solution)/shard_map/psum | solution.py:62
  708.6 1.0 convolution_subtract_fusion
  711.0 245.9 %all-reduce.13.cloned.1.call-done = f32[128,128]{0,1:T(8,128)} async-done(((f32[128,128]{0,1:T(8,128)}), f32[128,128]{0,1:T(8,128)}) %all-reduce.13.cloned.1.call-update) | async-done | bytes 65552 | tf_op jit(solution)/shard_map/psum | solution.py:69
  957.0 0.9 copy.30
  957.9 0.9 fusion.3
  958.8 11.7 %cholesky.55 = f32[128,128]{1,0:T(8,128)S(1)} custom-call(f32[128,128]{1,0:T(8,128)S(1)} %fusion.3), custom_call_target="Cholesky" | custom-call | tf_op jit(solution)/shard_map/jit(cholesky)/cholesky | solution.py:70
  971.1 0.7 fusion.1
  971.8 9.8 custom-call.7
  (51 shorter events, 7.3 us)
Async XLA Ops:
  6.5 3.5 copy-start
  6.5 156.3 %all-reduce.15.cloned.1.call-start = ((), (), s32[]{:S(2)}) async-start(), calls=%async_computation.8 | async-start | bytes 2097152 | tf_op jit(solution)/shard_map/psum | solution.py:43
  11.0 2.2 copy-start.3
  12.0 77.5 %copy-start.2 = (s32[2,128]{1,0:T(2,128)S(1)}, s32[2,128]{1,0:T(2,128)}, u32[]{:S(2)}) copy-start(s32[2,128]{1,0:T(2,128)} %param.13) | copy-start | bytes 3076
  13.2 185.3 %reduce-scatter.7.cloned.1.call-start = ((), (), s32[]{:S(2)}) async-start(), calls=%async_computation.6 | async-start | bytes 147456 | tf_op jit(solution)/shard_map/reduce_scatter | solution.py:51
  162.9 310.3 %copy-start.1 = (bf16[128,2048]{1,0:T(8,128)(2,1)S(1)}, bf16[128,2048]{1,0:T(8,128)(2,1)}, u32[]{:S(2)}) copy-start(bf16[128,2048]{1,0:T(8,128)(2,1)} %get-tuple-element.16) | copy-start | bytes 1572868
  165.2 281.7 %all-reduce.7.cloned.1.call-start = ((), (), s32[]{:S(2)}) async-start(), calls=%async_computation.2 | async-start | bytes 131072 | tf_op jit(solution)/shard_map/psum | solution.py:69
  200.7 405.8 %all-reduce.9.cloned.1.call-start = ((), (), s32[]{:S(2)}) async-start(), calls=%async_computation.3 | async-start | bytes 131072 | tf_op jit(solution)/shard_map/psum | solution.py:62
  473.1 169.4 %reduce-scatter.9.cloned.1.call-start = ((), (), s32[]{:S(2)}) async-start(), calls=%async_computation.7 | async-start | bytes 147456 | tf_op jit(solution)/shard_map/reduce_scatter | solution.py:51
  474.4 234.2 %all-reduce.11.cloned.1.call-start = ((), (), s32[]{:S(2)}) async-start(), calls=%async_computation.4 | async-start | bytes 131072 | tf_op jit(solution)/shard_map/psum | solution.py:62
  606.5 350.4 %all-reduce.13.cloned.1.call-start = ((), (), s32[]{:S(2)}) async-start(), calls=%async_computation.5 | async-start | bytes 131072 | tf_op jit(solution)/shard_map/psum | solution.py:69
Sparse Core Ops, SparseCore 0:
  13.3 149.5 all-reduce.14
  165.4 33.0 reduce-scatter.6
  204.0 242.8 all-reduce.6
  473.3 133.1 all-reduce.8
  608.8 33.6 reduce-scatter.8
  644.6 63.9 all-reduce.10
  714.1 242.7 all-reduce.12
